TPU v7x, 256 devices: a whole 4x4x8 slice. The times are simulated.
256 devices in a mesh: row: 16 (over x, y), col: 16 (over z, core).
Axes of the slice: x: 4, y: 4, z: 8, core: 2. Of those that a mesh axis runs over, the one named last changes fastest.
Arguments:
- anc_inverse: float32 [10240, 10240], P('row', 'col'), may hold values from -0.0625 to 0.0625
- lower_anc: float32 [10240, 3, 384], P('col', None, 'row'), may hold values from -1.5 to 1.5
- upper_anc: float32 [10240, 3, 384], P('row', None, 'col'), may hold values from -0.75 to 0.75
- lower_edge: float32 [2, 384, 384], replicated, may hold values from -0.3125 to 0.3125
- upper_edge: float32 [2, 384, 384], replicated, may hold values from -0.3125 to 0.3125
- diag_inverse: float32 [3, 384, 384], replicated, may hold values from -6 to 6
- tile_mask: int32 [3, 80, 3], replicated, may hold values 0 or 1
Outputs:
- x_blocks: float32 [10240, 3, 384], P(('row', 'col'))
- y_blocks: float32 [16, 16, 40, 3, 384], P('col', 'row')
- z_blocks: float32 [3, 384, 384], P(None, 'row', 'col')
- cross_blocks: float32 [2, 2, 384, 384], P(None, None, 'row', 'col')
All inputs are finite; a program needn't handle non-finite values.
Results may differ from a plain program's by a relative error of at most 0.0001.
Values sent between devices are 32-bit elements; how exact they have to be, the bound alone decides.
No kernel may reach another device: no remote copies, remote signals or barrier semaphores. Data moves between devices by JAX's collectives and lax.ppermute only.
A program may use at most 128 MiB of HBM per device.

v0:
```python
import jax
import jax.numpy as jnp
from jax import lax
from jax.sharding import PartitionSpec as P

W = 384
BLK = 128
SUPER = 3
precise = lax.Precision.HIGHEST


def product(left, right):
    return jnp.dot(left, right, precision=precise, preferred_element_type=jnp.float32)


def inner_product(left, right):
    return lax.dot_general(
        left, right, (((0,), (0,)), ((), ())), precision=precise, preferred_element_type=jnp.float32
    )


def outer_product(left, right):
    return lax.dot_general(
        left, right, (((1,), (1,)), ((), ())), precision=precise, preferred_element_type=jnp.float32
    )


def tile_pattern(tile_mask, first_block, blocks):
    window = lax.dynamic_slice_in_dim(tile_mask, first_block, blocks, 1).astype(jnp.float32)
    window = jnp.transpose(window, (1, 0, 2))
    widened = jnp.broadcast_to(window[:, None, :, :, None], (blocks, BLK, SUPER, W // BLK, BLK))
    return widened.reshape(blocks * BLK, SUPER, W)


def row_term(anc_inverse, lower_cols):
    return product(anc_inverse, lower_cols)


def col_term(anc_inverse, upper_rows):
    return inner_product(anc_inverse, upper_rows)


def per_device(anc_inverse, lower_anc, upper_anc, lower_edge, upper_edge, diag_inverse, tile_mask):
    rows_here, cols_here = anc_inverse.shape
    slab_rows = rows_here // lax.axis_size("col")
    row_index = lax.axis_index("row")
    col_index = lax.axis_index("col")
    col_pattern = tile_pattern(tile_mask, col_index * (cols_here // BLK), cols_here // BLK)
    row_pattern = tile_pattern(tile_mask, row_index * (rows_here // BLK), rows_here // BLK)
    lower_list = []
    upper_list = []
    cols_list = []
    rows_list = []
    for node_index in range(SUPER):
        lower_cur = (
            lax.all_gather(lower_anc[:, node_index, :], "row", axis=1, tiled=True)
            * col_pattern[:, node_index, :]
        )
        upper_cur = (
            lax.all_gather(upper_anc[:, node_index, :], "col", axis=1, tiled=True)
            * row_pattern[:, node_index, :]
        )
        lower_list.append(lower_cur)
        upper_list.append(upper_cur)
        cols_list.append(
            lax.psum_scatter(
                row_term(anc_inverse, lower_cur), "col", scatter_dimension=0, tiled=True
            )
        )
        rows_list.append(
            lax.psum_scatter(
                col_term(anc_inverse, upper_cur), "row", scatter_dimension=0, tiled=True
            )
        )
    x_list = []
    y_list = []
    corner_list = []
    cross_cols = []
    cross_rows = []
    for node_index in range(SUPER):
        lower_cur = lower_list[node_index]
        upper_cur = upper_list[node_index]
        inv_cols = -cols_list[node_index]
        inv_rows = -rows_list[node_index]
        upper_mine = lax.dynamic_slice_in_dim(upper_cur, col_index * slab_rows, slab_rows, 0)
        if node_index > 0:
            lower_side = lower_edge[node_index - 1]
            upper_side = upper_edge[node_index - 1]
            lower_mine = lax.dynamic_slice_in_dim(lower_cur, row_index * slab_rows, slab_rows, 0)
            rows_lower = inner_product(prev_rows, lower_mine)
            upper_cols = inner_product(upper_mine, prev_cols)
        if node_index > 0:
            rows_lower, upper_cols = lax.psum((rows_lower, upper_cols), ("row", "col"))
        if node_index > 0:
            cross_col = -(rows_lower + product(prev_corner, lower_side))
            cross_row = -(upper_cols + product(upper_side, prev_corner))
            inv_cols = inv_cols - product(prev_cols, lower_side)
            inv_rows = inv_rows - outer_product(prev_rows, upper_side)
            cross_cols.append(cross_col)
            cross_rows.append(cross_row)
        inv_corner = diag_inverse[node_index] - lax.psum(
            inner_product(upper_mine, inv_cols), ("row", "col")
        )
        if node_index > 0:
            inv_corner = inv_corner - product(upper_side, cross_col)
        x_list.append(inv_cols)
        y_list.append(inv_rows)
        corner_list.append(inv_corner)
        prev_cols = inv_cols
        prev_rows = inv_rows
        prev_corner = inv_corner
    x_blocks = jnp.stack(x_list, axis=1)
    y_blocks = jnp.stack(y_list, axis=1)[None, None]
    tile_rows = W // lax.axis_size("row")
    tile_cols = W // lax.axis_size("col")
    corners = jnp.stack(corner_list)
    corners = lax.dynamic_slice_in_dim(corners, row_index * tile_rows, tile_rows, 1)
    z_blocks = lax.dynamic_slice_in_dim(corners, col_index * tile_cols, tile_cols, 2)
    crossed = jnp.stack([jnp.stack(cross_cols), jnp.stack(cross_rows)])
    crossed = lax.dynamic_slice_in_dim(crossed, row_index * tile_rows, tile_rows, 2)
    cross_blocks = lax.dynamic_slice_in_dim(crossed, col_index * tile_cols, tile_cols, 3)
    return (x_blocks, y_blocks, z_blocks, cross_blocks)


def solution(mesh):
    return jax.shard_map(
        per_device,
        mesh=mesh,
        in_specs=(
            P("row", "col"),
            P("col", None, "row"),
            P("row", None, "col"),
            P(),
            P(),
            P(),
            P(),
        ),
        out_specs=(
            P(("row", "col"), None, None),
            P("col", "row", None, None, None),
            P(None, "row", "col"),
            P(None, None, "row", "col"),
        ),
        check_vma=False,
    )
```

profile of v0, /device:TPU:4, one launch (start us, length us, event | category | flops | bytes accessed | tf_op | source)
XLA Modules:
  0.0 653.5 jit_solution(15798240488232442538)
XLA Ops:
  8.3 26.5 %all-gather = f32[640,1,384]{0,1,2:T(1,128)} all-gather(f32[640,1,24]{0,1,2:T(1,128)S(1)} %copy.79), channel_id=2, replica_groups=mesh['row'=16,'col'=16] {'row'}, dimensions={2}, use_global_device_ids=true | all-gather | bytes 1044480 | tf_op jit(solution)/shard_map/all_gather | solution.py:56
  39.8 5.9 reshape.16
  45.7 24.7 %all-gather.2 = f32[640,1,384]{0,1,2:T(1,128)} all-gather(f32[640,1,24]{0,1,2:T(1,128)S(1)} %copy.81), channel_id=4, replica_groups=mesh['row'=16,'col'=16] {'row'}, dimensions={2}, use_global_device_ids=true | all-gather | bytes 1044480 | tf_op jit(solution)/shard_map/all_gather | solution.py:56
  70.5 3.2 copy.46
  73.8 25.1 %all-gather.1 = f32[640,1,384]{0,1,2:T(1,128)} all-gather(f32[640,1,24]{0,1,2:T(1,128)S(1)} %copy.80), channel_id=3, replica_groups=mesh['row'=16,'col'=16] {'row'}, dimensions={2}, use_global_device_ids=true | all-gather | bytes 1044480 | tf_op jit(solution)/shard_map/all_gather | solution.py:56
  98.9 3.7 copy.43
  102.7 7.1 %convolution_bitcast_fusion.5 = f32[640,384]{0,1:T(8,128)} fusion(f32[640,640]{1,0:T(8,128)S(1)} %copy-done, f32[640,1,384]{2,0,1:T(8,128)S(1)} %copy.41, f32[640,3,384]{2,0,1:T(8,128)} %reshape.16), kind=kOutput, calls=%fused_computation.10 | convolution fusion | flops 1887682560 | bytes 4587520 | tf_op jit(solution)/shard_map/dot_general | solution.py:13
  111.3 5.9 convolution_bitcast_fusion.4
  117.2 6.1 convolution_bitcast_fusion.3
  124.3 24.7 %all-gather.5 = f32[640,1,384]{0,1,2:T(1,128)} all-gather(f32[640,1,24]{0,1,2:T(1,128)S(1)} %copy.84), channel_id=7, replica_groups=mesh['row'=16,'col'=16] {'col'}, dimensions={2}, use_global_device_ids=true | all-gather | bytes 1044480 | tf_op jit(solution)/shard_map/all_gather | solution.py:60
  149.1 18.5 %all-gather.4 = f32[640,1,384]{0,1,2:T(1,128)S(1)} all-gather(f32[640,1,24]{0,1,2:T(1,128)S(1)} %copy.83), channel_id=6, replica_groups=mesh['row'=16,'col'=16] {'col'}, dimensions={2}, use_global_device_ids=true | all-gather | bytes 1044480 | tf_op jit(solution)/shard_map/all_gather | solution.py:60
  167.6 21.5 %all-gather.3 = f32[640,1,384]{0,1,2:T(1,128)} all-gather(f32[640,1,24]{0,1,2:T(1,128)S(1)} %copy.82), channel_id=5, replica_groups=mesh['row'=16,'col'=16] {'col'}, dimensions={2}, use_global_device_ids=true | all-gather | bytes 1044480 | tf_op jit(solution)/shard_map/all_gather | solution.py:60
  189.1 3.2 copy.56
  194.9 5.9 reshape.17
  202.7 3.3 copy.51
  206.0 2.7 slice_multiply_fusion
  208.8 3.9 convolution_bitcast_fusion.2
  212.7 3.9 convolution_bitcast_fusion.1
  216.6 3.9 convolution_bitcast_fusion
  223.7 21.6 %all-reduce.15.cloned.1.call-done = (f32[640,384]{0,1:T(8,128)}, f32[640,384]{0,1:T(8,128)}, f32[640,384]{0,1:T(8,128)}) async-done(((f32[640,384]{0,1:T(8,128)}, f32[640,384]{0,1:T(8,128)}, f32[640,384]{0,1:T(8,128)}), (f32[640,384]{0,1:T(8,128)}, f32[640,384]{0,1:T(8,128)}, f32[640,384]{0,1:T(8,128)})) %all-reduce.15.cloned.1.call-update) | async-done | bytes 2949136
  246.8 2.8 fusion.42
  249.6 2.9 fusion.41
  261.6 91.4 %all-reduce.17.cloned.1.call-done = (f32[640,384]{0,1:T(8,128)}, f32[640,384]{0,1:T(8,128)}, f32[640,384]{0,1:T(8,128)}) async-done(((f32[640,384]{0,1:T(8,128)}, f32[640,384]{0,1:T(8,128)}, f32[640,384]{0,1:T(8,128)}), (f32[640,384]{0,1:T(8,128)}, f32[640,384]{0,1:T(8,128)}, f32[640,384]{0,1:T(8,128)})) %all-reduce.17.cloned.1.call-update) | async-done | bytes 2949136
  366.8 267.0 %all-reduce.13.cloned.1.call-done = (f32[384,384]{1,0:T(8,128)}, f32[384,384]{1,0:T(8,128)}, f32[384,384]{1,0:T(8,128)}, f32[384,384]{1,0:T(8,128)}, f32[384,384...) async-done(((f32[384,384]{1,0:T(8,128)}, f32[384,384]{1,0:T(8,128)}, f32[384,384]{1,0:T(8,128)}, f32[384,384]{1,0:T(8,128)}, f32[384,384]{1,0:T(8,128)}, ...) | async-done | bytes 4128784 | tf_op jit(solution)/shard_map/psum | solution.py:93
  (105 shorter events, 52.1 us)
Async XLA Ops:
  7.2 95.5 %copy-start = (f32[640,640]{1,0:T(8,128)S(1)}, f32[640,640]{1,0:T(8,128)}, u32[]{:S(2)}) copy-start(f32[640,640]{1,0:T(8,128)} %param.7) | copy-start | bytes 4915204
  7.2 238.1 %all-reduce.15.cloned.1.call-start = ((), (), s32[]{:S(2)}) async-start(), calls=%async_computation.1 | async-start | bytes 5898240
  8.2 28.9 %copy-start.21 = (s32[3,80,3]{1,2,0:T(4,128)S(1)}, s32[3,80,3]{1,2,0:T(4,128)}, u32[]{:S(2)}) copy-start(s32[3,80,3]{1,2,0:T(4,128)} %param.13) | copy-start | bytes 8644
  102.7 7.1 %copy-start.1 = (f32[640,3,384]{2,0,1:T(8,128)S(1)}, f32[640,3,384]{2,0,1:T(8,128)}, u32[]{:S(2)}) copy-start(f32[640,3,384]{2,0,1:T(8,128)} %reshape.16) | copy-start | bytes 8847364
  102.7 7.1 %copy-start.14 = (f32[640,1,384]{2,0,1:T(8,128)S(1)}, f32[640,1,384]{2,0,1:T(8,128)}, u32[]{:S(2)}) copy-start(f32[640,1,384]{2,0,1:T(8,128)} %copy.46) | copy-start | bytes 2949124
  111.3 5.9 copy-start.11
  111.3 5.9 copy-start.10
  123.3 229.7 %all-reduce.17.cloned.1.call-start = ((), (), s32[]{:S(2)}) async-start(), calls=%async_computation.2 | async-start | bytes 5898240
  202.7 3.3 copy-start.13
  208.7 3.9 copy-start.12
  208.7 3.9 copy-start.9
  208.7 7.9 %copy-start.8 = (f32[640,1,384]{2,0,1:T(8,128)}, f32[640,1,384]{2,0,1:T(8,128)S(1)}, u32[]{:S(2)}) copy-start(f32[640,1,384]{2,0,1:T(8,128)S(1)} %get-tuple-element.25) | copy-start | bytes 2949124
  220.6 32.0 %copy-start.5 = (f32[2,384,384]{2,1,0:T(8,128)S(1)}, f32[2,384,384]{2,1,0:T(8,128)}, u32[]{:S(2)}) copy-start(f32[2,384,384]{2,1,0:T(8,128)} %param.10) | copy-start | bytes 3538948
  220.6 413.2 %all-reduce.13.cloned.1.call-start = ((), (), s32[]{:S(2)}) async-start(), calls=%async_computation | async-start | bytes 8257536 | tf_op jit(solution)/shard_map/psum | solution.py:93
  249.6 9.2 %copy-start.6 = (f32[2,384,384]{2,1,0:T(8,128)S(1)}, f32[2,384,384]{2,1,0:T(8,128)}, u32[]{:S(2)}) copy-start(f32[2,384,384]{2,1,0:T(8,128)} %param.10) | copy-start | bytes 3538948
  258.8 97.9 %copy-start.2 = (f32[2,384,384]{2,1,0:T(8,128)S(1)}, f32[2,384,384]{2,1,0:T(8,128)}, u32[]{:S(2)}) copy-start(f32[2,384,384]{2,1,0:T(8,128)} %param.11) | copy-start | bytes 3538948
  633.8 1.5 copy-start.3
  633.8 1.8 copy-start.7
  635.2 3.1 copy-start.4
  635.2 3.1 copy-start.19
  638.3 1.3 copy-start.18
  639.6 1.3 copy-start.17
  640.9 1.6 copy-start.16
  642.5 1.3 copy-start.15
  (3 other events, 2.9 us)
Sparse Core Ops, SparseCore 0:
  123.5 121.7 all-reduce.14
  249.0 103.9 all-reduce.16
  361.1 272.6 all-reduce.12
where the time goes:
time: 658 us; the launch traced here: 653 us
  waiting for transfers between devices  380 us (58%)
  blocking collectives  141 us (21%)
  matrix products  62.5 us (9%)
  local copies, waits for them, and re-layouts  42.9 us (7%)
  between operations  15.7 us (2%)
  other arithmetic  10.9 us (2%)
    psum x1, waiting for transfers between devices, per_device(): rows_lower, upper_cols = lax.psum((rows_lower, upper_cols), ('row', 'col'))  267 us
    unnamed x5, waiting for transfers between devices  113 us
    all_gather x3, blocking collectives, per_device(): lax.all_gather(lower_anc[:, node_index, :], 'row', axis=1, tiled=True)  76.4 us
    all_gather x3, blocking collectives, per_device(): lax.all_gather(upper_anc[:, node_index, :], 'col', axis=1, tiled=True)  64.6 us
    dot_general x11, matrix products, product(): jnp.dot(left, right, precision=precise, preferred_element_type=jnp.float32)  30.5 us
    dot_general x10, matrix products, inner_product(): lax.dot_general(left, right, (((0,), (0,)), ((), ())), precision=precise,...  29.4 us
  transfers between devices with their start and end apart: 3, of which 3 were waited for; matrix products, arithmetic and copies ran while one was open for 8% of the time, Pallas kernels for 0%

commit v1 on v0

--- a/solution.py
+++ b/solution.py
@@ -7,6 +7,24 @@
 BLK = 128
 SUPER = 3
 precise = lax.Precision.HIGHEST
+
+
+def gather_around(array, axis, dim):
+    ways, here, turn = (lax.axis_size(axis), lax.axis_index(axis), array.shape[dim])
+    lengths = [n * ways if d == dim else n for d, n in enumerate(array.shape)]
+    full = lax.dynamic_update_slice_in_dim(
+        jnp.zeros(lengths, array.dtype), array, here * turn, axis=dim
+    )
+    going_up = going_down = array
+    for far in range(1, ways // 2 + 1):
+        going_up = lax.ppermute(going_up, axis, [(d, (d + 1) % ways) for d in range(ways)])
+        full = lax.dynamic_update_slice_in_dim(full, going_up, (here - far) % ways * turn, axis=dim)
+        if 2 * far < ways:
+            going_down = lax.ppermute(going_down, axis, [(d, (d - 1) % ways) for d in range(ways)])
+            full = lax.dynamic_update_slice_in_dim(
+                full, going_down, (here + far) % ways * turn, axis=dim
+            )
+    return full
 
 
 def product(left, right):
@@ -57,8 +75,7 @@
             * col_pattern[:, node_index, :]
         )
         upper_cur = (
-            lax.all_gather(upper_anc[:, node_index, :], "col", axis=1, tiled=True)
-            * row_pattern[:, node_index, :]
+            gather_around(upper_anc[:, node_index, :], "col", 1) * row_pattern[:, node_index, :]
         )
         lower_list.append(lower_cur)
         upper_list.append(upper_cur)

time: 658 us -> 818 us (1.24)
  local copies, waits for them, and re-layouts: 42.9 us -> 222 us
  blocking collectives: 141 us -> 75.2 us
  starting transfers between devices: 0.33 us -> 59.2 us
  waiting for transfers between devices: 380 us -> 360 us
    dynamic_update_slice x0 -> x48, local copies, waits for them, and re-layouts: none -> 183 us  [the longest x24 87.1 us: gather_around(): lax.dynamic_update_slice_in_dim(full, going_up, (here - far) % ways * tur...]
    all_gather x3 -> x0, blocking collectives: 64.6 us -> none  [per_device(): lax.all_gather(upper_anc[:, node_index, :], 'col', axis=1, tiled=True)]
    ppermute x0 -> x45, starting transfers between devices: none -> 58.8 us  [the longest x21 58.2 us: gather_around(): lax.ppermute(going_down, axis, [(d, (d - 1) % ways) for d in range(ways)])]
    unnamed x5, waiting for transfers between devices: 113 us -> 83.2 us
    ppermute x0 -> x45, waiting for transfers between devices: none -> 10.1 us  [the longest x24 7.2 us: gather_around(): lax.ppermute(going_up, axis, [(d, (d + 1) % ways) for d in range(ways)])]
    all_gather x3 -> x0, local copies, waits for them, and re-layouts: 8.47 us -> none  [per_device(): lax.all_gather(upper_anc[:, node_index, :], 'col', axis=1, tiled=True)]
  transfers between devices with their start and end apart: 3 -> 48, of which waited for: 3 -> 6; matrix products, arithmetic and copies ran while one was open for 8% -> 34% of each run, Pallas kernels for 0% -> 0%
where the time goes in v1:
time: 818 us; the launch traced here: 808 us
  waiting for transfers between devices  360 us (44%)
  local copies, waits for them, and re-layouts  222 us (27%)
  blocking collectives  75.2 us (9%)
  matrix products  62.4 us (8%)
  starting transfers between devices  59.2 us (7%)
  between operations  16.4 us (2%)
  other arithmetic  12.6 us (2%)
    psum x1, waiting for transfers between devices, per_device(): rows_lower, upper_cols = lax.psum((rows_lower, upper_cols), ('row', 'col'))  267 us
    dynamic_update_slice x24, local copies, waits for them, and re-layouts, gather_around(): lax.dynamic_update_slice_in_dim(full, going_up, (here - far) % ways * tur...  87.1 us
    dynamic_update_slice x21, local copies, waits for them, and re-layouts, gather_around(): lax.dynamic_update_slice_in_dim(full, going_down, (here + far) % ways * t...  85 us
    unnamed x5, waiting for transfers between devices  83.2 us
    all_gather x3, blocking collectives, per_device(): lax.all_gather(lower_anc[:, node_index, :], 'row', axis=1, tiled=True)  75.2 us
    ppermute x21, starting transfers between devices, gather_around(): lax.ppermute(going_down, axis, [(d, (d - 1) % ways) for d in range(ways)])  58.2 us
    dot_general x11, matrix products, product(): jnp.dot(left, right, precision=precise, preferred_element_type=jnp.float32)  30.6 us
    dot_general x10, matrix products, inner_product(): lax.dot_general(left, right, (((0,), (0,)), ((), ())), precision=precise,...  29.3 us
  transfers between devices with their start and end apart: 48, of which 6 were waited for; matrix products, arithmetic and copies ran while one was open for 34% of the time, Pallas kernels for 0%

profile of v1, /device:TPU:4, one launch (start us, length us, event | category | flops | bytes accessed | tf_op | source)
XLA Modules:
  0.0 807.8 jit_solution(14514764023088938508)
XLA Ops:
  8.5 5.3 collective-permute-start.1
  17.9 24.7 %all-gather.1 = f32[640,1,384]{0,1,2:T(1,128)S(1)} all-gather(f32[640,1,24]{0,1,2:T(1,128)S(1)} %copy.77), channel_id=3, replica_groups=mesh['row'=16,'col'=16] {'row'}, dimensions={2}, use_global_device_ids=true | all-gather | bytes 1044480 | tf_op jit(solution)/shard_map/all_gather | solution.py:74
  42.8 25.0 %all-gather.2 = f32[640,1,384]{0,1,2:T(1,128)} all-gather(f32[640,1,24]{0,1,2:T(1,128)S(1)} %copy.78), channel_id=4, replica_groups=mesh['row'=16,'col'=16] {'row'}, dimensions={2}, use_global_device_ids=true | all-gather | bytes 1044480 | tf_op jit(solution)/shard_map/all_gather | solution.py:74
  76.4 5.9 reshape.16
  105.6 25.4 %all-gather = f32[640,1,384]{0,1,2:T(1,128)} all-gather(f32[640,1,24]{0,1,2:T(1,128)S(1)} %copy.76), channel_id=2, replica_groups=mesh['row'=16,'col'=16] {'row'}, dimensions={2}, use_global_device_ids=true | all-gather | bytes 1044480 | tf_op jit(solution)/shard_map/all_gather | solution.py:74
  140.4 7.3 convolution_bitcast_fusion.5
  156.6 5.8 convolution_bitcast_fusion.3
  169.0 6.3 convolution_bitcast_fusion.4
  192.0 4.3 collective-permute-done.42
  211.3 5.9 reshape.17
  235.0 4.4 dynamic_update_slice.178
  257.3 4.4 dynamic_update_slice.180
  279.6 4.4 dynamic_update_slice.182
  301.7 4.8 dynamic_update_slice.184
  324.5 4.7 dynamic_update_slice.186
  344.4 4.4 dynamic_update_slice.187
  348.8 4.4 dynamic_update_slice.188
  360.9 4.4 dynamic_update_slice.189
  372.8 4.4 dynamic_update_slice.190
  384.9 4.6 dynamic_update_slice.191
  392.2 3.9 convolution_bitcast_fusion
  396.1 3.9 convolution_bitcast_fusion.1
  423.4 83.2 %all-reduce.17.cloned.1.call-done = (f32[640,384]{0,1:T(8,128)}, f32[640,384]{0,1:T(8,128)}, f32[640,384]{0,1:T(8,128)}) async-done(((f32[640,384]{0,1:T(8,128)}, f32[640,384]{0,1:T(8,128)}, f32[640,384]{0,1:T(8,128)}), (f32[640,384]{0,1:T(8,128)}, f32[640,384]{0,1:T(8,128)}, f32[640,384]{0,1:T(8,128)})) %all-reduce.17.cloned.1.call-update) | async-done | bytes 2949136
  520.3 267.0 %all-reduce.13.cloned.1.call-done = (f32[384,384]{1,0:T(8,128)}, f32[384,384]{1,0:T(8,128)}, f32[384,384]{1,0:T(8,128)}, f32[384,384]{1,0:T(8,128)}, f32[384,384...) async-done(((f32[384,384]{1,0:T(8,128)}, f32[384,384]{1,0:T(8,128)}, f32[384,384]{1,0:T(8,128)}, f32[384,384]{1,0:T(8,128)}, f32[384,384]{1,0:T(8,128)}, ...) | async-done | bytes 4128784 | tf_op jit(solution)/shard_map/psum | solution.py:110
  (268 shorter events, 272.8 us)
Async XLA Ops:
  7.2 399.9 %all-reduce.15.cloned.1.call-start = ((), (), s32[]{:S(2)}) async-start(), calls=%async_computation.1 | async-start | bytes 5898240
  8.5 59.3 %collective-permute-start = (f32[640,24]{1,0:T(8,128)S(1)}, f32[640,24]{1,0:T(8,128)}, u32[]{:S(2)}, u32[]{:S(2)}) collective-permute-start(f32[640,24]{1,0:T(8,128)S(1)} %bitcast.175), channel_id=1, source_target_pairs={{0,1},{1,2},{2,3},{3,4},{4,5},{5,6},{6,7},{7,8},{8,9},{9,10},{10,1... | collective-permute-start | bytes 184328 | tf_op jit(solution)/shard_map/ppermute | solution.py:20
  8.5 59.3 %collective-permute-start.1 = (f32[640,24]{1,0:T(8,128)S(1)}, f32[640,24]{1,0:T(8,128)}, u32[]{:S(2)}, u32[]{:S(2)}) collective-permute-start(f32[640,24]{1,0:T(8,128)S(1)} %bitcast.176), channel_id=1, source_target_pairs={{0,15},{1,0},{2,1},{3,2},{4,3},{5,4},{6,5},{7,6},{8,7},{9,8},{10,9... | collective-permute-start | bytes 184328 | tf_op jit(solution)/shard_map/ppermute | solution.py:23
  14.0 54.3 %collective-permute-start.15 = (f32[640,24]{1,0:T(8,128)S(1)}, f32[640,24]{1,0:T(8,128)}, u32[]{:S(2)}, u32[]{:S(2)}) collective-permute-start(f32[640,24]{1,0:T(8,128)S(1)} %bitcast.178), channel_id=1, source_target_pairs={{0,1},{1,2},{2,3},{3,4},{4,5},{5,6},{6,7},{7,8},{8,9},{9,10},{10,1... | collective-permute-start | bytes 184328 | tf_op jit(solution)/shard_map/ppermute | solution.py:20
  14.0 56.8 %collective-permute-start.16 = (f32[640,24]{1,0:T(8,128)S(1)}, f32[640,24]{1,0:T(8,128)}, u32[]{:S(2)}, u32[]{:S(2)}) collective-permute-start(f32[640,24]{1,0:T(8,128)S(1)} %bitcast.179), channel_id=1, source_target_pairs={{0,15},{1,0},{2,1},{3,2},{4,3},{5,4},{6,5},{7,6},{8,7},{9,8},{10,9... | collective-permute-start | bytes 184328 | tf_op jit(solution)/shard_map/ppermute | solution.py:23
  17.9 53.0 %collective-permute-start.30 = (f32[640,24]{1,0:T(8,128)}, f32[640,24]{1,0:T(8,128)}, u32[]{:S(2)}, u32[]{:S(2)}) collective-permute-start(f32[640,24]{1,0:T(8,128)} %bitcast.22), channel_id=1, source_target_pairs={{0,1},{1,2},{2,3},{3,4},{4,5},{5,6},{6,7},{7,8},{8,9},{9,10},{10,1... | collective-permute-start | bytes 184328 | tf_op jit(solution)/shard_map/ppermute | solution.py:20
  67.8 19.6 %collective-permute-start.31 = (f32[640,24]{1,0:T(8,128)}, f32[640,24]{1,0:T(8,128)}, u32[]{:S(2)}, u32[]{:S(2)}) collective-permute-start(f32[640,24]{1,0:T(8,128)} %bitcast.22), channel_id=1, source_target_pairs={{0,15},{1,0},{2,1},{3,2},{4,3},{5,4},{6,5},{7,6},{8,7},{9,8},{10,9... | collective-permute-start | bytes 184328 | tf_op jit(solution)/shard_map/ppermute | solution.py:23
  67.8 19.6 %collective-permute-start.2 = (f32[640,24]{1,0:T(8,128)}, f32[640,24]{1,0:T(8,128)}, u32[]{:S(2)}, u32[]{:S(2)}) collective-permute-start(f32[640,24]{1,0:T(8,128)} %collective-permute-done), channel_id=1, source_target_pairs={{0,1},{1,2},{2,3},{3,4},{4,5},{5,6},{6,7},{7,8},{8,9},{9,10},{10,1... | collective-permute-start | bytes 184328 | tf_op jit(solution)/shard_map/ppermute | solution.py:20
  68.3 22.1 %collective-permute-start.3 = (f32[640,24]{1,0:T(8,128)}, f32[640,24]{1,0:T(8,128)}, u32[]{:S(2)}, u32[]{:S(2)}) collective-permute-start(f32[640,24]{1,0:T(8,128)} %collective-permute-done.1), channel_id=1, source_target_pairs={{0,15},{1,0},{2,1},{3,2},{4,3},{5,4},{6,5},{7,6},{8,7},{9,8},{10,9... | collective-permute-start | bytes 184328 | tf_op jit(solution)/shard_map/ppermute | solution.py:23
  70.8 19.6 %collective-permute-start.17 = (f32[640,24]{1,0:T(8,128)}, f32[640,24]{1,0:T(8,128)}, u32[]{:S(2)}, u32[]{:S(2)}) collective-permute-start(f32[640,24]{1,0:T(8,128)} %collective-permute-done.15), channel_id=1, source_target_pairs={{0,1},{1,2},{2,3},{3,4},{4,5},{5,6},{6,7},{7,8},{8,9},{9,10},{10,1... | collective-permute-start | bytes 184328 | tf_op jit(solution)/shard_map/ppermute | solution.py:20
  70.8 22.6 %collective-permute-start.18 = (f32[640,24]{1,0:T(8,128)}, f32[640,24]{1,0:T(8,128)}, u32[]{:S(2)}, u32[]{:S(2)}) collective-permute-start(f32[640,24]{1,0:T(8,128)} %collective-permute-done.16), channel_id=1, source_target_pairs={{0,15},{1,0},{2,1},{3,2},{4,3},{5,4},{6,5},{7,6},{8,7},{9,8},{10,9... | collective-permute-start | bytes 184328 | tf_op jit(solution)/shard_map/ppermute | solution.py:23
  96.7 37.8 %collective-permute-start.20 = (f32[640,24]{1,0:T(8,128)}, f32[640,24]{1,0:T(8,128)}, u32[]{:S(2)}, u32[]{:S(2)}) collective-permute-start(f32[640,24]{1,0:T(8,128)} %collective-permute-done.18), channel_id=1, source_target_pairs={{0,15},{1,0},{2,1},{3,2},{4,3},{5,4},{6,5},{7,6},{8,7},{9,8},{10,9... | collective-permute-start | bytes 184328 | tf_op jit(solution)/shard_map/ppermute | solution.py:23
  99.6 34.8 %collective-permute-start.34 = (f32[640,24]{1,0:T(8,128)}, f32[640,24]{1,0:T(8,128)}, u32[]{:S(2)}, u32[]{:S(2)}) collective-permute-start(f32[640,24]{1,0:T(8,128)} %collective-permute-done.32), channel_id=1, source_target_pairs={{0,1},{1,2},{2,3},{3,4},{4,5},{5,6},{6,7},{7,8},{8,9},{9,10},{10,1... | collective-permute-start | bytes 184328 | tf_op jit(solution)/shard_map/ppermute | solution.py:20
  99.6 37.8 %collective-permute-start.35 = (f32[640,24]{1,0:T(8,128)}, f32[640,24]{1,0:T(8,128)}, u32[]{:S(2)}, u32[]{:S(2)}) collective-permute-start(f32[640,24]{1,0:T(8,128)} %collective-permute-done.33), channel_id=1, source_target_pairs={{0,15},{1,0},{2,1},{3,2},{4,3},{5,4},{6,5},{7,6},{8,7},{9,8},{10,9... | collective-permute-start | bytes 184328 | tf_op jit(solution)/shard_map/ppermute | solution.py:23
  102.6 34.8 %collective-permute-start.6 = (f32[640,24]{1,0:T(8,128)}, f32[640,24]{1,0:T(8,128)}, u32[]{:S(2)}, u32[]{:S(2)}) collective-permute-start(f32[640,24]{1,0:T(8,128)} %collective-permute-done.4), channel_id=1, source_target_pairs={{0,1},{1,2},{2,3},{3,4},{4,5},{5,6},{6,7},{7,8},{8,9},{9,10},{10,1... | collective-permute-start | bytes 184328 | tf_op jit(solution)/shard_map/ppermute | solution.py:20
  102.6 37.8 %collective-permute-start.7 = (f32[640,24]{1,0:T(8,128)}, f32[640,24]{1,0:T(8,128)}, u32[]{:S(2)}, u32[]{:S(2)}) collective-permute-start(f32[640,24]{1,0:T(8,128)} %collective-permute-done.5), channel_id=1, source_target_pairs={{0,15},{1,0},{2,1},{3,2},{4,3},{5,4},{6,5},{7,6},{8,7},{9,8},{10,9... | collective-permute-start | bytes 184328 | tf_op jit(solution)/shard_map/ppermute | solution.py:23
  165.3 16.9 %collective-permute-start.26 = (f32[640,24]{1,0:T(8,128)}, f32[640,24]{1,0:T(8,128)}, u32[]{:S(2)}, u32[]{:S(2)}) collective-permute-start(f32[640,24]{1,0:T(8,128)} %collective-permute-done.24), channel_id=1, source_target_pairs={{0,15},{1,0},{2,1},{3,2},{4,3},{5,4},{6,5},{7,6},{8,7},{9,8},{10,9... | collective-permute-start | bytes 184328 | tf_op jit(solution)/shard_map/ppermute | solution.py:23
  175.4 331.2 %all-reduce.17.cloned.1.call-start = ((), (), s32[]{:S(2)}) async-start(), calls=%async_computation.2 | async-start | bytes 5898240
  183.8 185.1 %collective-permute-start.28 = (f32[640,24]{1,0:T(8,128)}, f32[640,24]{1,0:T(8,128)}, u32[]{:S(2)}, u32[]{:S(2)}) collective-permute-start(f32[640,24]{1,0:T(8,128)} %collective-permute-done.26), channel_id=1, source_target_pairs={{0,15},{1,0},{2,1},{3,2},{4,3},{5,4},{6,5},{7,6},{8,7},{9,8},{10,9... | collective-permute-start | bytes 184328 | tf_op jit(solution)/shard_map/ppermute | solution.py:23
  187.1 185.7 %collective-permute-start.43 = (f32[640,24]{1,0:T(8,128)}, f32[640,24]{1,0:T(8,128)}, u32[]{:S(2)}, u32[]{:S(2)}) collective-permute-start(f32[640,24]{1,0:T(8,128)} %collective-permute-done.41), channel_id=1, source_target_pairs={{0,15},{1,0},{2,1},{3,2},{4,3},{5,4},{6,5},{7,6},{8,7},{9,8},{10,9... | collective-permute-start | bytes 184328 | tf_op jit(solution)/shard_map/ppermute | solution.py:23
  189.2 188.1 %collective-permute-start.14 = (f32[640,24]{1,0:T(8,128)}, f32[640,24]{1,0:T(8,128)}, u32[]{:S(2)}, u32[]{:S(2)}) collective-permute-start(f32[640,24]{1,0:T(8,128)} %collective-permute-done.12), channel_id=1, source_target_pairs={{0,1},{1,2},{2,3},{3,4},{4,5},{5,6},{6,7},{7,8},{8,9},{9,10},{10,1... | collective-permute-start | bytes 184328 | tf_op jit(solution)/shard_map/ppermute | solution.py:20
  192.0 189.1 %collective-permute-start.29 = (f32[640,24]{1,0:T(8,128)}, f32[640,24]{1,0:T(8,128)}, u32[]{:S(2)}, u32[]{:S(2)}) collective-permute-start(f32[640,24]{1,0:T(8,128)} %collective-permute-done.27), channel_id=1, source_target_pairs={{0,1},{1,2},{2,3},{3,4},{4,5},{5,6},{6,7},{7,8},{8,9},{9,10},{10,1... | collective-permute-start | bytes 184328 | tf_op jit(solution)/shard_map/ppermute | solution.py:20
  196.3 188.6 %collective-permute-start.44 = (f32[640,24]{1,0:T(8,128)}, f32[640,24]{1,0:T(8,128)}, u32[]{:S(2)}, u32[]{:S(2)}) collective-permute-start(f32[640,24]{1,0:T(8,128)} %collective-permute-done.42), channel_id=1, source_target_pairs={{0,1},{1,2},{2,3},{3,4},{4,5},{5,6},{6,7},{7,8},{8,9},{9,10},{10,1... | collective-permute-start | bytes 184328 | tf_op jit(solution)/shard_map/ppermute | solution.py:20
  404.0 383.3 %all-reduce.13.cloned.1.call-start = ((), (), s32[]{:S(2)}) async-start(), calls=%async_computation | async-start | bytes 8257536 | tf_op jit(solution)/shard_map/psum | solution.py:110
  (62 other events, 912.4 us)
Sparse Core Ops, SparseCore 0:
  175.5 119.2 all-reduce.14
  404.1 102.4 all-reduce.16
  514.6 272.6 all-reduce.12
